TPU v7x, 128 devices: a whole 4x4x4 slice. The times are simulated.
128 devices in a mesh: seq: 8 (over x, core), chan: 16 (over y, z).
Axes of the slice: x: 4, y: 4, z: 4, core: 2. Of those that a mesh axis runs over, the one named last changes fastest.
Arguments:
- tokens: bfloat16 [6144, 8192], P('seq', 'chan'), may hold values from -6 to 6
- norm_gain: bfloat16 [8192], P('chan'), may hold values from 0.099609375 to 1.8984375
- in_weight: bfloat16 [8192, 3, 8192], P('seq', None, 'chan'), may hold values from -0.0625 to 0.0625
- conv_weight: bfloat16 [3, 3, 8192], P(None, None, 'chan'), may hold values from -3 to 3
- filters: bfloat16 [512, 128], P('chan'), may hold values from -0.5 to 0.5
- out_weight: bfloat16 [8192, 8192], P('chan'), may hold values from -0.09375 to 0.09375
Outputs:
- result: bfloat16 [6144, 8192], P('seq', 'chan')
All inputs are finite; a program needn't handle non-finite values.
Results may differ from a plain program's by a relative error of at most 0.0084.
Values may be sent and summed in bfloat16 or wider, within the bound.
A program may use at most 192 MiB of HBM per device.

v0:
```python
import jax
import jax.numpy as jnp
import numpy as np
from jax import lax
from jax.sharding import PartitionSpec as P


def lag_table(filters):
    groups, length = filters.shape
    width = 3 * length
    zeros = jnp.zeros((groups, length), filters.dtype)
    skew = jnp.concatenate([zeros, filters[:, ::-1], zeros], axis=1)
    tiled = jnp.tile(skew, (1, length + 1))[:, : length * (width + 1)]
    windows = tiled.reshape(groups, length, width + 1)[:, :, : 2 * length]
    return windows[:, ::-1, :]


def hyena_core(extended, conv_weight, filters):
    length = filters.shape[1]
    values = extended.astype(jnp.float32)
    weights = conv_weight.astype(jnp.float32)
    shaped = (
        weights[:, 0, :] * values[2:]
        + weights[:, 1, :] * values[1:-1]
        + weights[:, 2, :] * values[:-2]
    )
    total = shaped.shape[0]
    out_rows = total - length
    query = shaped[length:, 0, :]
    mixed = (shaped[:, 1, :] * shaped[:, 2, :]).astype(jnp.bfloat16)
    group_count = filters.shape[0]
    channel_count = mixed.shape[1]
    blocks = mixed.reshape(total // length, length, group_count, channel_count // group_count)
    paired = jnp.concatenate([blocks[:-1], blocks[1:]], axis=1)
    table = lag_table(filters)
    filtered = jnp.einsum("gts,bsgw->btgw", table, paired, preferred_element_type=jnp.float32)
    filtered = filtered.reshape(out_rows, channel_count)
    return (query * filtered).astype(jnp.bfloat16)


def local(tokens, norm_gain, in_weight, conv_weight, filters, out_weight):
    row_count = tokens.shape[0]
    chan_count = in_weight.shape[2]
    length = filters.shape[1]
    joined = jnp.concatenate([tokens, norm_gain[None, :]], axis=0)
    whole_joined = lax.all_gather(joined, "chan", axis=1, tiled=True)
    whole, gain_whole = (whole_joined[:row_count], whole_joined[row_count])
    values = whole.astype(jnp.float32)
    mean_square = jnp.mean(values * values, axis=1, keepdims=True)
    normed = (values * lax.rsqrt(mean_square + 1e-06) * gain_whole.astype(jnp.float32)).astype(
        jnp.bfloat16
    )
    piece = lax.all_gather(in_weight, "seq", axis=0, tiled=True)
    panel = piece.reshape(piece.shape[0], 3 * chan_count)
    projected = jnp.dot(normed, panel, preferred_element_type=jnp.float32)
    streams = projected.astype(jnp.bfloat16).reshape(row_count, 3, chan_count)
    parts_count = lax.axis_size("seq")
    halo_rows = length + 2
    shift = [(i, i + 1) for i in range(parts_count - 1)]
    halo = lax.ppermute(streams[row_count - halo_rows :], "seq", shift)
    extended = jnp.concatenate([halo, streams], axis=0)
    gated = hyena_core(extended, conv_weight, filters)
    partial_out = jnp.dot(gated, out_weight, preferred_element_type=jnp.float32)
    summed = lax.psum_scatter(partial_out, "chan", scatter_dimension=1, tiled=True)
    return (tokens.astype(jnp.float32) + summed).astype(jnp.bfloat16)


def solution(mesh):
    return jax.shard_map(
        local,
        mesh=mesh,
        in_specs=(
            P("seq", "chan"),
            P("chan"),
            P("seq", None, "chan"),
            P(None, None, "chan"),
            P("chan", None),
            P("chan", None),
        ),
        out_specs=P("seq", "chan"),
        check_vma=False,
    )
```

profile of v0, /device:TPU:1, one launch (start us, length us, event | category | flops | bytes accessed | tf_op | source)
XLA Modules:
  0.0 496.6 jit_solution(15601686603221840330)
XLA Ops:
  7.2 2.1 pad_maximum_fusion
  9.4 4.6 copy.13
  14.1 96.5 %all-gather.3.cloned.1.call-done = bf16[769,8192]{1,0:T(8,128)(2,1)} async-done(((bf16[769,512]{1,0:T(8,128)(2,1)}), bf16[769,8192]{1,0:T(8,128)(2,1)}) %all-gather.3.cloned.1.call-update) | async-done | bytes 12599312 | tf_op jit(solution)/shard_map/all_gather | solution.py:46
  110.6 7.1 %fusion = f32[768]{0:T(1024)S(1)} fusion(bf16[769,8192]{1,0:T(8,128)(2,1)} %all-gather.3.cloned.1.call-done), kind=kLoop, calls=%fused_computation.2 | loop fusion | flops 18873600 | bytes 12585984 | tf_op jit(solution)/shard_map/reduce_sum | solution.py:49
  118.7 114.9 %all-gather.5.cloned.1.call-done = bf16[8192,3,512]{0,2,1:T(8,128)(2,1)} async-done(((bf16[1024,3,512]{0,2,1:T(8,128)(2,1)}), bf16[8192,3,512]{0,2,1:T(8,128)(2,1)}) %all-gather.5.cloned.1.call-update) | async-done | bytes 25165840 | tf_op jit(solution)/shard_map/all_gather | solution.py:53
  233.5 27.1 %fusion.10 = bf16[768,1536]{1,0:T(8,128)(2,1)S(1)} fusion(bf16[8192,1536]{0,1:T(8,128)(2,1)} %bitcast.49, f32[8192]{0:T(1024)S(1)} %bitcast.48, f32[768]{0:T(1024)S(1)} %add_rsqrt_fusion, bf16[769,8192]{1,0:T(8,128)(2,1)} %all-gather.3.cloned.1.call-done), kind=kOutput, calls=%fused_computation.14 | convolution fusion | flops 19353698304 | bytes 40143872 | tf_op jit(solution)/shard_map/dot_general | solution.py:55
  261.1 1.1 copy.14
  262.2 3.4 collective-permute-start
  266.7 8.9 %reshape.39 = bf16[32,128,385]{2,1,0:T(8,128)(2,1)} reshape(bf16[32,49280]{1,0:T(8,128)(2,1)S(1)} %slice.92) | data formatting | bytes 6307840 | tf_op jit(solution)/shard_map/reshape | solution.py:14
  275.6 1.6 slice-done.2
  277.2 20.2 %rev.7 = bf16[32,128,256]{2,1,0:T(8,128)(2,1)} reverse(bf16[32,128,256]{2,1,0:T(8,128)(2,1)S(1)} %slice-done.2), dimensions={1} | reverse | bytes 4194304 | tf_op jit(solution)/shard_map/rev | solution.py:15
  297.4 2.8 copy.15
  300.3 1.3 copy.16
  301.6 1.3 maximum_convert_fusion
  302.9 4.5 fusion.8
  307.4 2.4 copy-done
  310.0 1.3 fusion.28
  311.3 2.0 slice.73
  313.2 1.0 copy.17
  314.3 2.0 slice.75
  316.4 2.1 fusion.20
  319.1 15.5 %fusion.25 = f32[768,8192]{1,0:T(8,128)} fusion(bf16[512,8192]{1,0:T(8,128)(2,1)} %param.11, f32[64,8,6,128]{3,2,1,0:T(8,128)S(1)} %bitcast.44, f32[896,3,512]{0,2,1:T(8,128)S(1)} %bitcast.42), kind=kOutput, calls=%fused_computation.29 | convolution fusion | flops 6443237376 | bytes 37224448 | tf_op jit(solution)/shard_map/dot_general | solution.py:63
  334.6 152.9 %reduce-scatter.2.cloned.1.call-done = f32[768,512]{1,0:T(8,128)} async-done(((f32[768,8192]{1,0:T(8,128)}), f32[768,512]{1,0:T(8,128)}) %reduce-scatter.2.cloned.1.call-update) | async-done | bytes 1572880 | tf_op jit(solution)/shard_map/reduce_scatter | solution.py:64
  487.5 2.5 add_convert_fusion
  (41 shorter events, 4.1 us)
Async XLA Ops:
  6.5 104.1 %all-gather.3.cloned.1.call-start = ((), (), s32[]{:S(2)}) async-start(), calls=%async_computation.1 | async-start | bytes 13508608 | tf_op jit(solution)/shard_map/all_gather | solution.py:46
  9.3 224.2 %all-gather.5.cloned.1.call-start = ((), (), s32[]{:S(2)}) async-start(), calls=%async_computation.2 | async-start | bytes 28311552 | tf_op jit(solution)/shard_map/all_gather | solution.py:53
  14.1 473.4 %reduce-scatter.2.cloned.1.call-start = ((), (), s32[]{:S(2)}) async-start(), calls=%async_computation.3 | async-start | bytes 26738688 | tf_op jit(solution)/shard_map/reduce_scatter | solution.py:64
  233.5 32.1 %copy-start.4 = (bf16[3,3,512]{2,1,0:T(4,128)(2,1)S(1)}, bf16[3,3,512]{2,1,0:T(4,128)(2,1)}, u32[]{:S(2)}) copy-start(bf16[3,3,512]{2,1,0:T(4,128)(2,1)} %param.9) | copy-start | bytes 27652
  233.5 32.1 %copy-start.5 = (bf16[32,128]{1,0:T(8,128)(2,1)S(1)}, bf16[32,128]{1,0:T(8,128)(2,1)}, u32[]{:S(2)}) copy-start(bf16[32,128]{1,0:T(8,128)(2,1)} %param.10) | copy-start | bytes 24580
  260.7 5.8 %copy-start.2 = (bf16[768,1536]{1,0:T(8,128)(2,1)}, bf16[768,1536]{1,0:T(8,128)(2,1)S(1)}, u32[]{:S(2)}) copy-start(bf16[768,1536]{1,0:T(8,128)(2,1)S(1)} %fusion.10) | copy-start | bytes 7077892
  262.2 38.1 %collective-permute-start = (bf16[130,3,512]{2,0,1:T(8,128)(2,1)}, bf16[130,3,512]{2,0,1:T(8,128)(2,1)}, u32[]{:S(2)}, u32[]{:S(2)}) collective-permute-start(bf16[130,3,512]{2,0,1:T(8,128)(2,1)} %copy.14), channel_id=1, source_target_pairs={{0,16},{16,32},{32,48},{48,64},{64,80},{80,96},{96,112},{1,17},{17... | collective-permute-start | bytes 1198088 | tf_op jit(solution)/shard_map/ppermute | solution.py:60
  275.6 1.6 slice-start.2
  307.4 2.4 copy-start
  310.0 6.4 %copy-start.1 = (bf16[32,128,256]{2,1,0:T(8,128)(2,1)S(1)}, bf16[32,128,256]{2,1,0:T(8,128)(2,1)}, u32[]{:S(2)}) copy-start(bf16[32,128,256]{2,1,0:T(8,128)(2,1)} %rev.7) | copy-start | bytes 6291460
  316.2 2.9 slice-start
  316.4 2.7 slice-start.1
  334.6 152.9 %copy-start.3 = (bf16[768,512]{1,0:T(8,128)(2,1)S(1)}, bf16[768,512]{1,0:T(8,128)(2,1)}, u32[]{:S(2)}) copy-start(bf16[768,512]{1,0:T(8,128)(2,1)} %param.6) | copy-start | bytes 2359300
Sparse Core Ops, SparseCore 0:
  9.5 101.1 all-gather.2
  112.3 121.1 all-gather.4
  334.8 152.6 reduce-scatter.1
where the time goes:
time: 497 us
  waiting for transfers between devices  364 us (73%)
  local copies, waits for them, and re-layouts  52.1 us (10%)
  matrix products  44.7 us (9%)
  other arithmetic  18.7 us (4%)
  between operations  13.4 us (3%)
    reduce_scatter x1, waiting for transfers between devices, local(): lax.psum_scatter(partial_out, 'chan', scatter_dimension=1, tiled=True)  153 us
    all_gather x1, waiting for transfers between devices, local(): piece = lax.all_gather(in_weight, 'seq', axis=0, tiled=True)  115 us
    all_gather x1, waiting for transfers between devices, local(): whole_joined = lax.all_gather(joined, 'chan', axis=1, tiled=True)  96.5 us
    dot_general x1, matrix products, local(): projected = jnp.dot(normed, panel, preferred_element_type=jnp.float32)  27.1 us
    rev x1, local copies, waits for them, and re-layouts, lag_table(): return windows[:, ::-1, :]  20.2 us
    dot_general x1, matrix products, local(): partial_out = jnp.dot(gated, out_weight, preferred_element_type=jnp.float32)  15.5 us
  transfers between devices with their start and end apart: 4, of which 3 were waited for; matrix products, arithmetic and copies ran while one was open for 9% of the time, Pallas kernels for 0%

commit v1 on v0

--- a/solution.py
+++ b/solution.py
@@ -50,7 +50,9 @@
     normed = (values * lax.rsqrt(mean_square + 1e-06) * gain_whole.astype(jnp.float32)).astype(
         jnp.bfloat16
     )
-    piece = lax.all_gather(in_weight, "seq", axis=0, tiled=True)
+    piece = jnp.concatenate(
+        lax.all_to_all(jnp.stack([in_weight] * lax.axis_size("seq")), "seq", 0, 0), axis=0
+    )
     panel = piece.reshape(piece.shape[0], 3 * chan_count)
     projected = jnp.dot(normed, panel, preferred_element_type=jnp.float32)
     streams = projected.astype(jnp.bfloat16).reshape(row_count, 3, chan_count)

time: 497 us -> 589 us (1.19)
  local copies, waits for them, and re-layouts: 52.1 us -> 101 us
  waiting for transfers between devices: 364 us -> 399 us
  starting transfers between devices: 3.48 us -> 11 us
    all_to_all x0 -> x1, waiting for transfers between devices: none -> 242 us  [local(): lax.all_to_all(jnp.stack([in_weight] * lax.axis_size('seq')), 'seq', 0, 0)]
    all_gather x1 -> x0, waiting for transfers between devices: 115 us -> none  [local(): piece = lax.all_gather(in_weight, 'seq', axis=0, tiled=True)]
    all_gather x1, waiting for transfers between devices: 96.5 us -> 0.01 us  [local(): whole_joined = lax.all_gather(joined, 'chan', axis=1, tiled=True)]
    all_to_all x0 -> x1, local copies, waits for them, and re-layouts: none -> 22.4 us  [local(): lax.all_to_all(jnp.stack([in_weight] * lax.axis_size('seq')), 'seq', 0, 0)]
    unnamed x20 -> x21, local copies, waits for them, and re-layouts: 7.5 us -> 26.3 us
    another operation x0 -> x1, local copies, waits for them, and re-layouts: none -> 8.66 us  [local(): jnp.stack([in_weight] * lax.axis_size('seq'))]
    all_to_all x0 -> x1, starting transfers between devices: none -> 7.98 us  [local(): lax.all_to_all(jnp.stack([in_weight] * lax.axis_size('seq')), 'seq', 0, 0)]
  transfers between devices with their start and end apart: 4 -> 4, of which waited for: 3 -> 3; matrix products, arithmetic and copies ran while one was open for 9% -> 15% of each run, Pallas kernels for 0% -> 0%
where the time goes in v1:
time: 589 us; the launch traced here: 588 us
  waiting for transfers between devices  399 us (68%)
  local copies, waits for them, and re-layouts  101 us (17%)
  matrix products  44.6 us (8%)
  other arithmetic  18.6 us (3%)
  between operations  13.7 us (2%)
  starting transfers between devices  11 us (2%)
    all_to_all x1, waiting for transfers between devices, local(): lax.all_to_all(jnp.stack([in_weight] * lax.axis_size('seq')), 'seq', 0, 0)  242 us
    reduce_scatter x1, waiting for transfers between devices, local(): lax.psum_scatter(partial_out, 'chan', scatter_dimension=1, tiled=True)  156 us
    dot_general x1, matrix products, local(): projected = jnp.dot(normed, panel, preferred_element_type=jnp.float32)  27.3 us
    unnamed x21, local copies, waits for them, and re-layouts  26.3 us
    all_to_all x1, local copies, waits for them, and re-layouts, local(): lax.all_to_all(jnp.stack([in_weight] * lax.axis_size('seq')), 'seq', 0, 0)  22.4 us
    rev x1, local copies, waits for them, and re-layouts, lag_table(): return windows[:, ::-1, :]  20.3 us
    dot_general x1, matrix products, local(): partial_out = jnp.dot(gated, out_weight, preferred_element_type=jnp.float32)  15.3 us
  transfers between devices with their start and end apart: 4, of which 3 were waited for; matrix products, arithmetic and copies ran while one was open for 15% of the time, Pallas kernels for 0%

profile of v1, /device:TPU:1, one launch (start us, length us, event | category | flops | bytes accessed | tf_op | source)
XLA Modules:
  0.0 588.3 jit_solution(15304223125656335441)
XLA Ops:
  7.2 2.1 pad_maximum_fusion
  9.3 3.2 copy.14
  12.5 8.7 %stack.2 = bf16[8,1024,3,512]{1,3,2,0:T(8,128)(2,1)} broadcast(bf16[1024,3,512]{0,2,1:T(8,128)(2,1)S(1)} %copy.14), dimensions={1,2,3} | broadcast | bytes 28311552 | tf_op jit(solution)/shard_map/stack | solution.py:54
  21.2 8.0 %all-to-all-start = ((bf16[8,1024,3,512]{1,3,2,0:T(8,128)(2,1)}), bf16[8,1024,3,512]{1,3,2,0:T(8,128)(2,1)}, u32[]{:S(2)}, u32[]{:S(2)}) async-start(bf16[8,1024,3,512]{1,3,2,0:T(8,128)(2,1)} %stack.2), calls=%async_computation | async-start | bytes 50331648 | tf_op jit(solution)/shard_map/all_to_all | solution.py:54
  30.2 8.9 %reshape.37 = bf16[32,128,385]{2,1,0:T(8,128)(2,1)} reshape(bf16[32,49280]{1,0:T(8,128)(2,1)S(1)} %slice.92) | data formatting | bytes 6307840 | tf_op jit(solution)/shard_map/reshape | solution.py:14
  39.1 1.6 slice-done.2
  40.7 20.3 %rev.7 = bf16[32,128,256]{2,1,0:T(8,128)(2,1)} reverse(bf16[32,128,256]{2,1,0:T(8,128)(2,1)S(1)} %slice-done.2), dimensions={1} | reverse | bytes 4194304 | tf_op jit(solution)/shard_map/rev | solution.py:15
  61.0 241.6 %all-to-all-done = bf16[8,1024,3,512]{1,3,2,0:T(8,128)(2,1)} async-done(((bf16[8,1024,3,512]{1,3,2,0:T(8,128)(2,1)}), bf16[8,1024,3,512]{1,3,2,0:T(8,128)(2,1)}, u32[]{:S(2)}, u32[]{:S(2)}) %all-to-all-start) | async-done | bytes 25165856 | tf_op jit(solution)/shard_map/all_to_all | solution.py:54
  302.7 22.4 %copy.15 = bf16[8,1024,3,512]{1,0,3,2:T(8,128)(2,1)S(1)} copy(bf16[8,1024,3,512]{1,3,2,0:T(8,128)(2,1)} %all-to-all-done) | data formatting | bytes 50331648 | tf_op jit(solution)/shard_map/all_to_all | solution.py:54
  325.0 20.2 %copy.26 = bf16[192,8,8,1024]{3,1,2,0:T(8,128)(2,1)} copy(bf16[192,8,8,1024]{3,2,1,0:T(8,128)(2,1)S(1)} %bitcast.45) | data formatting | bytes 50331648
  345.3 7.1 %fusion = f32[768]{0:T(1024)S(1)} fusion(bf16[769,8192]{1,0:T(8,128)(2,1)} %all-gather.2.cloned.1.call-done), kind=kLoop, calls=%fused_computation.2 | loop fusion | flops 18873600 | bytes 12585984 | tf_op jit(solution)/shard_map/reduce_sum | solution.py:49
  353.3 27.3 %fusion.10 = bf16[768,1536]{1,0:T(8,128)(2,1)S(1)} fusion(bf16[8192,1536]{0,1:T(8,128)(2,1)} %bitcast.48, f32[8192]{0:T(1024)S(1)} %bitcast.54, f32[768]{0:T(1024)S(1)} %add_rsqrt_fusion, bf16[769,8192]{1,0:T(8,128)(2,1)} %all-gather.2.cloned.1.call-done), kind=kOutput, calls=%fused_computation.14 | convolution fusion | flops 19353698304 | bytes 40143872 | tf_op jit(solution)/shard_map/dot_general | solution.py:57
  381.1 3.0 collective-permute-start
  384.3 3.1 copy.17
  387.3 1.8 collective-permute-done
  390.4 1.3 maximum_convert_fusion
  391.7 4.5 fusion.8
  396.3 2.4 copy-done
  400.2 2.0 slice.75
  403.2 2.0 slice.73
  405.3 2.1 fusion.20
  408.0 15.3 %fusion.25 = f32[768,8192]{1,0:T(8,128)} fusion(bf16[512,8192]{1,0:T(8,128)(2,1)} %param.11, f32[64,8,6,128]{3,2,1,0:T(8,128)S(1)} %bitcast.50, f32[896,3,512]{0,2,1:T(8,128)S(1)} %bitcast.47), kind=kOutput, calls=%fused_computation.29 | convolution fusion | flops 6443237376 | bytes 37224448 | tf_op jit(solution)/shard_map/dot_general | solution.py:65
  423.3 155.6 %reduce-scatter.2.cloned.1.call-done = f32[768,512]{1,0:T(8,128)} async-done(((f32[768,8192]{1,0:T(8,128)}), f32[768,512]{1,0:T(8,128)}) %reduce-scatter.2.cloned.1.call-update) | async-done | bytes 1572880 | tf_op jit(solution)/shard_map/reduce_scatter | solution.py:66
  578.9 2.5 add_convert_fusion
  (43 shorter events, 7.7 us)
Async XLA Ops:
  6.5 338.7 %all-gather.2.cloned.1.call-start = ((), (), s32[]{:S(2)}) async-start(), calls=%async_computation.2 | async-start | bytes 13508608 | tf_op jit(solution)/shard_map/all_gather | solution.py:46
  21.2 8.0 %copy-start.5 = (bf16[32,128]{1,0:T(8,128)(2,1)S(1)}, bf16[32,128]{1,0:T(8,128)(2,1)}, u32[]{:S(2)}) copy-start(bf16[32,128]{1,0:T(8,128)(2,1)} %param.10) | copy-start | bytes 24580
  21.2 281.5 %all-to-all-start = ((bf16[8,1024,3,512]{1,3,2,0:T(8,128)(2,1)}), bf16[8,1024,3,512]{1,3,2,0:T(8,128)(2,1)}, u32[]{:S(2)}, u32[]{:S(2)}) async-start(bf16[8,1024,3,512]{1,3,2,0:T(8,128)(2,1)} %stack.2), calls=%async_computation | async-start | bytes 50331648 | tf_op jit(solution)/shard_map/all_to_all | solution.py:54
  29.1 549.8 %reduce-scatter.2.cloned.1.call-start = ((), (), s32[]{:S(2)}) async-start(), calls=%async_computation.3 | async-start | bytes 26738688 | tf_op jit(solution)/shard_map/reduce_scatter | solution.py:66
  39.1 1.6 slice-start.2
  353.3 30.9 %copy-start.4 = (bf16[3,3,512]{2,1,0:T(4,128)(2,1)S(1)}, bf16[3,3,512]{2,1,0:T(4,128)(2,1)}, u32[]{:S(2)}) copy-start(bf16[3,3,512]{2,1,0:T(4,128)(2,1)} %param.9) | copy-start | bytes 27652
  380.6 3.6 copy-start.2
  381.1 8.0 %collective-permute-start = (bf16[130,3,512]{2,0,1:T(8,128)(2,1)S(1)}, bf16[130,3,512]{2,0,1:T(8,128)(2,1)}, u32[]{:S(2)}, u32[]{:S(2)}) collective-permute-start(bf16[130,3,512]{2,0,1:T(8,128)(2,1)S(1)} %copy.16), channel_id=1, source_target_pairs={{0,16},{16,32},{32,48},{48,64},{64,80},{80,96},{96,112},{1,17},{17... | collective-permute-start | bytes 1198088 | tf_op jit(solution)/shard_map/ppermute | solution.py:62
  396.3 2.4 copy-start
  398.9 6.4 %copy-start.1 = (bf16[32,128,256]{2,1,0:T(8,128)(2,1)S(1)}, bf16[32,128,256]{2,1,0:T(8,128)(2,1)}, u32[]{:S(2)}) copy-start(bf16[32,128,256]{2,1,0:T(8,128)(2,1)} %rev.7) | copy-start | bytes 6291460
  405.1 2.9 slice-start
  405.3 2.7 slice-start.1
  423.3 155.6 %copy-start.3 = (bf16[768,512]{1,0:T(8,128)(2,1)S(1)}, bf16[768,512]{1,0:T(8,128)(2,1)}, u32[]{:S(2)}) copy-start(bf16[768,512]{1,0:T(8,128)(2,1)} %param.6) | copy-start | bytes 2359300
Sparse Core Ops, SparseCore 0:
  9.4 101.1 all-gather.1
  423.4 155.4 reduce-scatter.1
